TPU v7x, 512 devices: a whole 4x4x16 slice. The times are simulated.
512 devices in a mesh: gx: 4 (over y), gy: 16 (over z_lo, core), ha: 8 (over x, z_hi).
Axes of the slice: x: 4, y: 4, z: 16 (z_hi: 2, z_lo: 8; z = z_hi * 8 + z_lo), core: 2. Of those that a mesh axis runs over, the one named last changes fastest.
Arguments:
- value: float32 [4, 64, 128, 512], P(None, 'ha', 'gy', 'gx'), may hold values from -6 to 6
- obstacles: float32 [5, 128], replicated, may hold values from -1 to 1
- obstacle_slots: int32 [16, 16], P('ha'), may hold values from 0 to 127
- horizon: float32 [1], replicated, may hold values from 0.5 to 2
- speed_offset: int32 [1], replicated, may hold values from 2 to 11
Outputs:
- next_value: float32 [4, 64, 128, 512], P(None, 'ha', 'gy', 'gx')
Inputs may be any that keep to these rules, and one draw needn't show every extreme that they name: `obstacle_slots`: each heading group of 4 headings lists 16 obstacle numbers, repeats allowed.
All inputs are finite; a program needn't handle non-finite values.
Results may differ from a plain program's by a relative error of at most 0.00002.
Values sent between devices are 32-bit elements; how exact they have to be, the bound alone decides.
A program may use at most 64 MiB of HBM per device.

v0:
```python
import math

import jax
import jax.numpy as jnp
from jax import lax
from jax.sharding import PartitionSpec as P

GH = 4


cfl_number = 0.75
weno_eps = 1e-06
half_width = 20.0
speed_step = 0.5
turn_limit = 1.0
accel_limit = 4.0
obstacle_speed = 2.0
car_radius = 0.8
body_offsets = (-1.0, 0.0, 1.0)


def extended_2(value, sides, width, wrap):
    for axis, dim in sides:
        count, length = (lax.axis_size(axis), value.shape[dim])
        up = [(i, (i + 1) % count) for i in range(count if wrap else count - 1)]
        down = [(j, i) for i, j in up]
        last = lax.slice_in_dim(value, length - width, length, axis=dim)
        initial = lax.slice_in_dim(value, 0, width, axis=dim)
        before = lax.ppermute(last, axis, up)
        after = lax.ppermute(initial, axis, down)
        value = jnp.concatenate([before, value, after], axis=dim)
    return value


def weno_side(outer_diff, middle_diff, inner_diff):
    weight_one = 1.0 / 3.0 / jnp.square(weno_eps + jnp.square(middle_diff - outer_diff))
    weight_two = 2.0 / 3.0 / jnp.square(weno_eps + jnp.square(inner_diff - middle_diff))
    return (
        weight_one * (1.5 * middle_diff - 0.5 * outer_diff)
        + weight_two * (0.5 * middle_diff + 0.5 * inner_diff)
    ) / (weight_one + weight_two)


def slopes(padded, along_dim, spacing):
    length = padded.shape[along_dim] - 4
    samples = [
        lax.slice_in_dim(padded, offset_idx, offset_idx + length, axis=along_dim)
        for offset_idx in range(5)
    ]
    back_far = (samples[1] - samples[0]) / spacing
    back_near = (samples[2] - samples[1]) / spacing
    ahead_near = (samples[3] - samples[2]) / spacing
    ahead_far = (samples[4] - samples[3]) / spacing
    return (weno_side(back_far, back_near, ahead_near), weno_side(ahead_far, ahead_near, back_near))


def hamiltonian_rate(pieces, speeds, angles, spreads, spacings):
    speed_minus, speed_plus = slopes(pieces[0], 0, spacings[0])
    head_minus, head_plus = slopes(pieces[1], 1, spacings[1])
    y_minus, y_plus = slopes(pieces[2], 2, spacings[2])
    x_minus, x_plus = slopes(pieces[3], 3, spacings[3])
    along_x = speeds[:, None, None, None] * jnp.cos(angles)[None, :, None, None]
    along_y = speeds[:, None, None, None] * jnp.sin(angles)[None, :, None, None]
    hamilton = along_x * (0.5 * (x_minus + x_plus)) + along_y * (0.5 * (y_minus + y_plus))
    hamilton = (
        hamilton
        + turn_limit * jnp.abs(0.5 * (head_minus + head_plus))
        + accel_limit * jnp.abs(0.5 * (speed_minus + speed_plus))
    )
    damping = spreads[0] * (x_plus - x_minus) + spreads[1] * (y_plus - y_minus)
    damping = (
        damping + turn_limit * (head_plus - head_minus) + accel_limit * (speed_plus - speed_minus)
    )
    return jnp.minimum(0.0, hamilton - 0.5 * damping)


def speed_bounds(speeds, angles, step_x, step_y):
    along_x = jnp.abs(speeds[:, None] * jnp.cos(angles)[None, :])
    along_y = jnp.abs(speeds[:, None] * jnp.sin(angles)[None, :])
    return (jnp.max(along_x), jnp.max(along_y), jnp.max(along_x / step_x + along_y / step_y))


def group_field(obstacles, horizon, step_time, x_cells, y_cells, angle_group, slot_row):
    moment = horizon[0] + step_time
    centre_x = half_width * obstacles[0] + moment * (obstacle_speed * obstacles[2])
    centre_y = half_width * obstacles[1] + moment * (obstacle_speed * obstacles[3])
    reach = 1.25 + 0.75 * obstacles[4] + car_radius
    centre_x = jnp.take(centre_x, slot_row)[None, :, None, None]
    centre_y = jnp.take(centre_y, slot_row)[None, :, None, None]
    reach = jnp.take(reach, slot_row)[None, :, None, None]
    cosine = jnp.cos(angle_group)[:, None, None, None]
    sine = jnp.sin(angle_group)[:, None, None, None]
    nearest = None
    for offset in body_offsets:
        moved_x = x_cells[None, None, None, :] + offset * cosine
        moved_y = y_cells[None, None, :, None] + offset * sine
        clearance = (
            jnp.sqrt(jnp.square(moved_x - centre_x) + jnp.square(moved_y - centre_y)) - reach
        )
        closest = jnp.min(clearance, axis=1)
        nearest = closest if nearest is None else jnp.minimum(nearest, closest)
    return nearest


def clamp_edges(extended, margin):
    span_x = extended.shape[3]
    span_y = extended.shape[2]
    column_ids = lax.broadcasted_iota(jnp.int32, (1, 1, 1, span_x), 3)
    left_edge = jnp.logical_and(column_ids < margin, lax.axis_index("gx") == 0)
    right_edge = jnp.logical_and(
        column_ids >= span_x - margin, lax.axis_index("gx") == lax.axis_size("gx") - 1
    )
    extended = jnp.where(left_edge, extended[:, :, :, margin : margin + 1], extended)
    extended = jnp.where(
        right_edge, extended[:, :, :, span_x - margin - 1 : span_x - margin], extended
    )
    row_ids = lax.broadcasted_iota(jnp.int32, (1, 1, span_y, 1), 2)
    lower_edge = jnp.logical_and(row_ids < margin, lax.axis_index("gy") == 0)
    upper_edge = jnp.logical_and(
        row_ids >= span_y - margin, lax.axis_index("gy") == lax.axis_size("gy") - 1
    )
    extended = jnp.where(lower_edge, extended[:, :, margin : margin + 1, :], extended)
    extended = jnp.where(
        upper_edge, extended[:, :, span_y - margin - 1 : span_y - margin, :], extended
    )
    return extended


def heading_angles(offset_id, length, local_heads, total_heads):
    indices = (
        lax.axis_index("ha") * local_heads + offset_id + jnp.arange(length, dtype=jnp.int32)
    ) % total_heads
    return indices.astype(jnp.float32) * (2.0 * math.pi / total_heads) - math.pi


def local(value, obstacles, obstacle_slots, horizon, speed_offset):
    speed_count, local_heads, local_rows, local_cols = value.shape
    total_heads = local_heads * lax.axis_size("ha")
    step_x = 2.0 * half_width / (local_cols * lax.axis_size("gx"))
    step_y = 2.0 * half_width / (local_rows * lax.axis_size("gy"))
    step_h = 2.0 * math.pi / total_heads
    speeds = speed_step * (
        speed_offset.astype(jnp.float32)[0] + jnp.arange(speed_count, dtype=jnp.float32)
    )
    own_angles = heading_angles(0, local_heads, local_heads, total_heads)
    whole_angles = jnp.arange(total_heads, dtype=jnp.int32).astype(jnp.float32) * step_h - math.pi
    spread_x, spread_y, fastest = speed_bounds(speeds, whole_angles, step_x, step_y)
    rate_total = fastest + turn_limit / step_h + accel_limit / speed_step
    time_step = cfl_number / rate_total
    spacings = (speed_step, step_h, step_y, step_x)

    def advance_box(extended, margin_out):
        inner = extended[:, 2:-2, 2:-2, 2:-2]
        pieces = (
            jnp.pad(inner, ((2, 2), (0, 0), (0, 0), (0, 0)), mode="edge"),
            extended[:, :, 2:-2, 2:-2],
            extended[:, 2:-2, :, 2:-2],
            extended[:, 2:-2, 2:-2, :],
        )
        angles = heading_angles(-margin_out, local_heads + 2 * margin_out, local_heads, total_heads)
        return inner + time_step * hamiltonian_rate(
            pieces, speeds, angles, (spread_x, spread_y), spacings
        )

    heading_ext = extended_2(value, (("ha", 1),), 4, True)
    extended = extended_2(heading_ext, (("gx", 3), ("gy", 2)), 4, False)
    extended = clamp_edges(extended, 4)
    section_one = clamp_edges(advance_box(extended, 2), 2)
    section_two = advance_box(section_one, 0)
    column_cells = (
        lax.axis_index("gx") * local_cols + jnp.arange(local_cols, dtype=jnp.int32)
    ).astype(jnp.float32)
    row_cells = (
        lax.axis_index("gy") * local_rows + jnp.arange(local_rows, dtype=jnp.int32)
    ).astype(jnp.float32)
    x_cells = (column_cells + 0.5) * step_x - half_width
    y_cells = (row_cells + 0.5) * step_y - half_width

    def one_group(packed):
        return group_field(obstacles, horizon, time_step, x_cells, y_cells, packed[0], packed[1])

    groups_local = local_heads // GH
    failure = lax.map(one_group, (own_angles.reshape(groups_local, GH), obstacle_slots))
    failure = failure.reshape(local_heads, local_rows, local_cols)
    return jnp.minimum(0.5 * (value + section_two), failure[None])


def solution(mesh):
    in_specs = (P(None, "ha", "gy", "gx"), P(), P("ha", None), P(), P())
    out_specs = P(None, "ha", "gy", "gx")
    return jax.shard_map(local, mesh=mesh, in_specs=in_specs, out_specs=out_specs, check_vma=False)
```

profile of v0, /device:TPU:1, one launch (start us, length us, event | category | flops | bytes accessed | tf_op | source)
XLA Modules:
  0.0 85.7 jit_solution(3759024732500965770)
XLA Ops:
  0.0 0.9 %fusion.103 = (f32[4,4,8,128]{3,2,1,0:T(8,128)S(1)}, f32[4,4,8,128]{3,2,1,0:T(8,128)S(1)}) fusion(f32[4,8,8,128]{3,2,1,0:T(8,128)} %param.9), kind=kLoop, calls=%fused_computation.234 | loop fusion | bytes 262144 | tf_op jit(solution)/shard_map/slice | solution.py:28
  0.9 16.3 %collective-permute-start = (f32[4,4,8,128]{3,2,1,0:T(8,128)S(1)}, f32[4,4,8,128]{3,2,1,0:T(8,128)S(1)}, u32[]{:S(2)}, u32[]{:S(2)}) collective-permute-start(f32[4,4,8,128]{3,2,1,0:T(8,128)S(1)} %get-tuple-element.226), channel_id=1, source_target_pairs={{0,1},{1,2},{2,3},{3,4},{4,5},{5,6},{6,7},{7,0},{8,9},{9,10},{10,1... | collective-permute-start | bytes 196616 | tf_op jit(solution)/shard_map/ppermute | solution.py:29
  17.2 4.1 %collective-permute-start.1 = (f32[4,4,8,128]{3,2,1,0:T(8,128)S(1)}, f32[4,4,8,128]{3,2,1,0:T(8,128)S(1)}, u32[]{:S(2)}, u32[]{:S(2)}) collective-permute-start(f32[4,4,8,128]{3,2,1,0:T(8,128)S(1)} %get-tuple-element.225), channel_id=1, source_target_pairs={{1,0},{2,1},{3,2},{4,3},{5,4},{6,5},{7,6},{0,7},{9,8},{10,9},{11,1... | collective-permute-start | bytes 196616 | tf_op jit(solution)/shard_map/ppermute | solution.py:30
  22.9 0.7 add_reduce_fusion
  24.2 8.9 %while.14 = (s32[]{:T(128)}, f32[2,4,8,128]{3,2,1,0:T(8,128)S(1)}, f32[2,4]{1,0:T(2,128)S(1)}, f32[5,128]{1,0:T(8,128)}, f32[]{:T(128)}, /*index=5*/s32[2,16]{1,0:T(2,128)}, s32[]{:T(128)}, s32[]{:T(128)}, s32[]{:T(128)}) while((s32[]{:T(128)}, f32[2,4,8,128]{3,2,1,0:T(8,128)S(1)}, f32[2,4]{1,0:T(2,128)S(1)}, f32[5,128]{1,0:T(8,128)}, ...), condition=%wide.region_7.9_spmd.clone, body=%wide.region_3.8_spmd.clone.sunk | while | flops 642522 | bytes 348229 | solution.py:183
  24.2 0.8 compare_select_fusion.8
  25.0 0.9 %add_bitcast_fusion.4 = (f32[128]{0:T(128)S(1)}, f32[128]{0:T(128)S(1)}, f32[128]{0:T(128)S(1)}) fusion(f32[5,128]{1,0:T(8,128)} %get-tuple-element.363, f32[]{:T(128)} %get-tuple-element.364), kind=kLoop, calls=%fused_computation.29.clone.1 | loop fusion | flops 1024 | bytes 4100 | tf_op jit(solution)/shard_map/while/body/eval_jaxpr/add | solution.py:87
  25.8 0.7 gather_fusion.1
  26.5 0.7 gather_fusion.2
  27.2 0.7 gather_fusion
  28.0 0.1 subtract_multiply_fusion.17
  28.1 0.1 broadcast_add_fusion.8
  28.2 0.1 subtract_multiply_fusion.16
  28.3 0.3 subtract_reduce_fusion.4
  28.6 0.8 compare_select_fusion.8
  29.4 0.9 %add_bitcast_fusion.4 = (f32[128]{0:T(128)S(1)}, f32[128]{0:T(128)S(1)}, f32[128]{0:T(128)S(1)}) fusion(f32[5,128]{1,0:T(8,128)} %get-tuple-element.363, f32[]{:T(128)} %get-tuple-element.364), kind=kLoop, calls=%fused_computation.29.clone.1 | loop fusion | flops 1024 | bytes 4100 | tf_op jit(solution)/shard_map/while/body/eval_jaxpr/add | solution.py:87
  30.3 0.7 gather_fusion.1
  30.9 0.7 gather_fusion.2
  31.6 0.7 gather_fusion
  32.4 0.1 broadcast_add_fusion.9
  32.5 0.1 subtract_multiply_fusion.17
  32.6 0.1 subtract_multiply_fusion.16
  32.7 0.3 subtract_reduce_fusion.4
  33.3 0.1 fusion.102
  33.4 3.2 %collective-permute-start.2 = (f32[4,16,8,4]{3,2,1,0:T(8,128)S(1)}, f32[4,16,8,4]{3,2,1,0:T(8,128)S(1)}, u32[]{:S(2)}, u32[]{:S(2)}) collective-permute-start(f32[4,16,8,4]{3,2,1,0:T(8,128)S(1)} %get-tuple-element.223), channel_id=1, source_target_pairs={{0,128},{128,256},{256,384},{1,129},{129,257},{257,385},{2,130},{1... | collective-permute-start | bytes 24584 | tf_op jit(solution)/shard_map/ppermute | solution.py:29
  36.7 1.3 %collective-permute-start.3 = (f32[4,16,8,4]{3,2,1,0:T(8,128)S(1)}, f32[4,16,8,4]{3,2,1,0:T(8,128)S(1)}, u32[]{:S(2)}, u32[]{:S(2)}) collective-permute-start(f32[4,16,8,4]{3,2,1,0:T(8,128)S(1)} %get-tuple-element.224), channel_id=1, source_target_pairs={{128,0},{256,128},{384,256},{129,1},{257,129},{385,257},{130,2},{2... | collective-permute-start | bytes 24584 | tf_op jit(solution)/shard_map/ppermute | solution.py:30
  38.0 3.4 %collective-permute-done.2 = f32[4,16,8,4]{3,2,1,0:T(8,128)S(1)} collective-permute-done((f32[4,16,8,4]{3,2,1,0:T(8,128)S(1)}, f32[4,16,8,4]{3,2,1,0:T(8,128)S(1)}, u32[]{:S(2)}, u32[]{:S(2)}) %collective-permute-start.2) | collective-permute-done | bytes 8224 | tf_op jit(solution)/shard_map/ppermute | solution.py:29
  41.3 3.8 %collective-permute-done.3 = f32[4,16,8,4]{3,2,1,0:T(8,128)S(1)} collective-permute-done((f32[4,16,8,4]{3,2,1,0:T(8,128)S(1)}, f32[4,16,8,4]{3,2,1,0:T(8,128)S(1)}, u32[]{:S(2)}, u32[]{:S(2)}) %collective-permute-start.3) | collective-permute-done | bytes 8224 | tf_op jit(solution)/shard_map/ppermute | solution.py:30
  45.2 0.3 pad_maximum_fusion.2
  45.5 0.1 fusion.101
  45.6 4.6 %collective-permute-start.4 = (f32[4,16,4,136]{3,1,2,0:T(8,128)S(1)}, f32[4,16,4,136]{3,1,2,0:T(8,128)S(1)}, u32[]{:S(2)}, u32[]{:S(2)}) collective-permute-start(f32[4,16,4,136]{3,1,2,0:T(8,128)S(1)} %copy.154), channel_id=1, source_target_pairs={{0,8},{8,16},{16,24},{24,32},{32,40},{40,48},{48,56},{56,64},{64,7... | collective-permute-start | bytes 417800 | tf_op jit(solution)/shard_map/ppermute | solution.py:29
  50.3 1.9 %collective-permute-start.5 = (f32[4,16,4,136]{3,1,2,0:T(8,128)S(1)}, f32[4,16,4,136]{3,1,2,0:T(8,128)S(1)}, u32[]{:S(2)}, u32[]{:S(2)}) collective-permute-start(f32[4,16,4,136]{3,1,2,0:T(8,128)S(1)} %copy.155), channel_id=1, source_target_pairs={{8,0},{16,8},{24,16},{32,24},{40,32},{48,40},{56,48},{64,56},{72,6... | collective-permute-start | bytes 417800 | tf_op jit(solution)/shard_map/ppermute | solution.py:30
  52.3 1.3 %collective-permute-done.4 = f32[4,16,4,136]{3,1,2,0:T(8,128)S(1)} collective-permute-done((f32[4,16,4,136]{3,1,2,0:T(8,128)S(1)}, f32[4,16,4,136]{3,1,2,0:T(8,128)S(1)}, u32[]{:S(2)}, u32[]{:S(2)}) %collective-permute-start.4) | collective-permute-done | bytes 139296 | tf_op jit(solution)/shard_map/ppermute | solution.py:29
  53.5 0.2 copy_dynamic-update-slice_fusion.2
  53.7 0.4 copy_dynamic-update-slice_fusion
  54.1 3.9 %collective-permute-done.5 = f32[4,16,4,136]{3,1,2,0:T(8,128)S(1)} collective-permute-done((f32[4,16,4,136]{3,1,2,0:T(8,128)S(1)}, f32[4,16,4,136]{3,1,2,0:T(8,128)S(1)}, u32[]{:S(2)}, u32[]{:S(2)}) %collective-permute-start.5) | collective-permute-done | bytes 139296 | tf_op jit(solution)/shard_map/ppermute | solution.py:30
  58.0 0.2 copy_dynamic-update-slice_fusion.1
  58.2 0.3 slice.330
  58.5 1.6 %copy.148 = f32[4,16,16,1]{0,2,1,3:T(8,128)S(1)} copy(f32[4,16,16,1]{3,0,2,1:T(4,128)S(1)} %slice.330) | data formatting | bytes 8192 | tf_op jit(solution)/shard_map/jit(_where)/broadcast_in_dim | solution.py:113
  60.2 0.3 broadcast_select_fusion.6
  60.5 0.3 slice.331
  60.8 1.6 %copy.149 = f32[4,16,16,1]{0,2,1,3:T(8,128)S(1)} copy(f32[4,16,16,1]{3,0,2,1:T(4,128)S(1)} %slice.331) | data formatting | bytes 8192 | tf_op jit(solution)/shard_map/jit(_where)/broadcast_in_dim | solution.py:114
  62.5 0.7 broadcast_select_fusion.5
  63.2 0.7 broadcast_select_fusion.4
  64.0 0.8 broadcast_select_fusion.3
  64.7 0.7 fusion.99
  65.4 0.4 slice.334
  65.8 0.1 reshape.591
  66.0 0.1 reshape.592
  66.1 11.8 %multiply_add_fusion.2 = f32[4,12,12,132]{3,0,2,1:T(4,128)S(1)} fusion(f32[4,12,12,132]{3,0,2,1:T(4,128)S(1)} %slice.334, f32[2,12,12,132]{3,0,2,1:T(2,128)S(1)} %reshape.592, f32[2,12,12,132]{3,0,2,1:T(2,128)S(1)} %reshape.591, f32[4,16,16,136]{3,0,2,1:T(4,128)S(1)} %broadcast_select_fusion.3, f32[]{:T(128)} %get-tuple-element.174, f32[]{:T(128)} %get-tuple-element.173, ...), kind=kLoop, calls=%fused_computation.60 | loop fusion | flops 16270848 | bytes 4562316 | tf_op jit(solution)/shard_map/add | solution.py:161
  77.9 0.2 slice.353
  78.1 0.4 copy.141
  78.5 0.2 copy.142
  78.7 0.2 broadcast_select_fusion.10
  78.9 0.2 slice.354
  79.2 0.4 copy.143
  79.5 0.2 copy.144
  79.7 0.4 broadcast_select_fusion.9
  80.1 0.4 broadcast_select_fusion.8
  80.5 0.4 broadcast_select_fusion.7
  80.9 0.2 fusion.100
  81.1 0.1 slice.357
  81.3 3.7 %fusion.46 = f32[4,8,8,128]{3,0,2,1:T(4,128)S(1)} fusion(f32[4,8,8,128]{3,2,1,0:T(8,128)S(1)} %copy-done, f32[4,8,8,128]{3,0,2,1:T(4,128)S(1)} %slice.357, f32[2,8,8,128]{3,0,2,1:T(2,128)S(1)} %reshape.594, f32[2,8,8,128]{3,0,2,1:T(2,128)S(1)} %reshape.593, f32[4,12,12,132]{3,0,2,1:T(4,128)S(1)} %broadcast_select_fusion.7, f32[]{:T(128)S(6)} %div.259, ...), kind=kLoop, calls=%fused_computation.133 | loop fusion | flops 7110656 | bytes 2130188 | tf_op jit(solution)/shard_map/min | solution.py:185
  85.0 0.7 copy.147
  (52 shorter events, 1.0 us)
Async XLA Ops:
  0.9 32.4 %collective-permute-start = (f32[4,4,8,128]{3,2,1,0:T(8,128)S(1)}, f32[4,4,8,128]{3,2,1,0:T(8,128)S(1)}, u32[]{:S(2)}, u32[]{:S(2)}) collective-permute-start(f32[4,4,8,128]{3,2,1,0:T(8,128)S(1)} %get-tuple-element.226), channel_id=1, source_target_pairs={{0,1},{1,2},{2,3},{3,4},{4,5},{5,6},{6,7},{7,0},{8,9},{9,10},{10,1... | collective-permute-start | bytes 196616 | tf_op jit(solution)/shard_map/ppermute | solution.py:29
  17.2 16.1 %collective-permute-start.1 = (f32[4,4,8,128]{3,2,1,0:T(8,128)S(1)}, f32[4,4,8,128]{3,2,1,0:T(8,128)S(1)}, u32[]{:S(2)}, u32[]{:S(2)}) collective-permute-start(f32[4,4,8,128]{3,2,1,0:T(8,128)S(1)} %get-tuple-element.225), channel_id=1, source_target_pairs={{1,0},{2,1},{3,2},{4,3},{5,4},{6,5},{7,6},{0,7},{9,8},{10,9},{11,1... | collective-permute-start | bytes 196616 | tf_op jit(solution)/shard_map/ppermute | solution.py:30
  24.2 9.1 %copy-start = (f32[4,8,8,128]{3,2,1,0:T(8,128)S(1)}, f32[4,8,8,128]{3,2,1,0:T(8,128)}, u32[]{:S(2)}) copy-start(f32[4,8,8,128]{3,2,1,0:T(8,128)} %param.9) | copy-start | bytes 393220
  24.2 3.6 %copy-start.1 = (s32[2,16]{1,0:T(2,128)S(1)}, s32[2,16]{1,0:T(2,128)}, u32[]{:S(2)}) copy-start(s32[2,16]{1,0:T(2,128)} %get-tuple-element.365) | copy-start | bytes 388 | tf_op jit(solution)/shard_map/while
  28.6 3.6 %copy-start.1 = (s32[2,16]{1,0:T(2,128)S(1)}, s32[2,16]{1,0:T(2,128)}, u32[]{:S(2)}) copy-start(s32[2,16]{1,0:T(2,128)} %get-tuple-element.365) | copy-start | bytes 388 | tf_op jit(solution)/shard_map/while
  33.4 7.9 %collective-permute-start.2 = (f32[4,16,8,4]{3,2,1,0:T(8,128)S(1)}, f32[4,16,8,4]{3,2,1,0:T(8,128)S(1)}, u32[]{:S(2)}, u32[]{:S(2)}) collective-permute-start(f32[4,16,8,4]{3,2,1,0:T(8,128)S(1)} %get-tuple-element.223), channel_id=1, source_target_pairs={{0,128},{128,256},{256,384},{1,129},{129,257},{257,385},{2,130},{1... | collective-permute-start | bytes 24584 | tf_op jit(solution)/shard_map/ppermute | solution.py:29
  36.7 8.5 %collective-permute-start.3 = (f32[4,16,8,4]{3,2,1,0:T(8,128)S(1)}, f32[4,16,8,4]{3,2,1,0:T(8,128)S(1)}, u32[]{:S(2)}, u32[]{:S(2)}) collective-permute-start(f32[4,16,8,4]{3,2,1,0:T(8,128)S(1)} %get-tuple-element.224), channel_id=1, source_target_pairs={{128,0},{256,128},{384,256},{129,1},{257,129},{385,257},{130,2},{2... | collective-permute-start | bytes 24584 | tf_op jit(solution)/shard_map/ppermute | solution.py:30
  45.6 7.9 %collective-permute-start.4 = (f32[4,16,4,136]{3,1,2,0:T(8,128)S(1)}, f32[4,16,4,136]{3,1,2,0:T(8,128)S(1)}, u32[]{:S(2)}, u32[]{:S(2)}) collective-permute-start(f32[4,16,4,136]{3,1,2,0:T(8,128)S(1)} %copy.154), channel_id=1, source_target_pairs={{0,8},{8,16},{16,24},{24,32},{32,40},{40,48},{48,56},{56,64},{64,7... | collective-permute-start | bytes 417800 | tf_op jit(solution)/shard_map/ppermute | solution.py:29
  50.3 7.7 %collective-permute-start.5 = (f32[4,16,4,136]{3,1,2,0:T(8,128)S(1)}, f32[4,16,4,136]{3,1,2,0:T(8,128)S(1)}, u32[]{:S(2)}, u32[]{:S(2)}) collective-permute-start(f32[4,16,4,136]{3,1,2,0:T(8,128)S(1)} %copy.155), channel_id=1, source_target_pairs={{8,0},{16,8},{24,16},{32,24},{40,32},{48,40},{56,48},{64,56},{72,6... | collective-permute-start | bytes 417800 | tf_op jit(solution)/shard_map/ppermute | solution.py:30
where the time goes:
time: 86.1 us; the launch traced here: 85.7 us
  starting transfers between devices  31.4 us (36%)
  other arithmetic  25.6 us (30%)
  local copies, waits for them, and re-layouts  13.8 us (16%)
  waiting for transfers between devices  12.4 us (14%)
  between operations  2.32 us (3%)
    ppermute x3, starting transfers between devices, extended_2(): before = lax.ppermute(last, axis, up)  24.1 us
    add x1, other arithmetic, advance_box(): inner + time_step * hamiltonian_rate(pieces, speeds, angles, (spread_x, s...  11.8 us
    ppermute x3, waiting for transfers between devices, extended_2(): after = lax.ppermute(initial, axis, down)  7.77 us
    ppermute x3, starting transfers between devices, extended_2(): after = lax.ppermute(initial, axis, down)  7.33 us
    ppermute x3, waiting for transfers between devices, extended_2(): before = lax.ppermute(last, axis, up)  4.64 us
    min x1, other arithmetic, local(): return jnp.minimum(0.5 * (value + section_two), failure[None])  3.68 us
    broadcast_in_dim x2, local copies, waits for them, and re-layouts, clamp_edges(): jnp.where(left_edge, extended[:, :, :, margin:margin + 1], extended)  1.78 us
    broadcast_in_dim x2, local copies, waits for them, and re-layouts, clamp_edges(): jnp.where(right_edge, extended[:, :, :, span_x - margin - 1:span_x - marg...  1.78 us
  transfers between devices with their start and end apart: 6, of which 4 were waited for; matrix products, arithmetic and copies ran while one was open for 12% of the time, Pallas kernels for 0%

commit v1 on v0

v1 whole, which is shorter than its diff:
```python
import functools
import math

import jax
import jax.numpy as jnp
import numpy as np
from jax import lax
from jax.experimental import pallas as pl
from jax.experimental.pallas import tpu as pltpu
from jax.sharding import PartitionSpec as P

MESH = pl.DeviceIdType.MESH
f32 = jnp.float32

cfl_number = 0.75
weno_eps = 1e-06
half_width = 20.0
speed_step = 0.5
turn_limit = 1.0
accel_limit = 4.0
obstacle_speed = 2.0
car_radius = 0.8
SLOTS = 16


def grid_tables(heads):
    step = np.float32(2.0 * math.pi / heads)
    angles = np.arange(heads, dtype=np.float32) * step - np.float32(math.pi)
    wide = angles.astype(np.float64)
    return np.cos(wide).astype(np.float32), np.sin(wide).astype(np.float32)


def sides(m2, m1, z0, p1, p2, eps):
    d1, d2, d3, d4 = m1 - m2, z0 - m1, p1 - z0, p2 - p1
    u, v, w = d2 - d1, d3 - d2, d4 - d3
    a, b, c = eps + u * u, eps + v * v, eps + w * w
    a, b, c = a * a, b * b, c * c
    p, q = b + (a + a), b + (c + c)
    r = b / (p * q)
    return p1 - m1, r, (u - v) * q, (w - v) * p


def upwind(parts, ca, cp, cm):
    dm, r, x, y = parts
    return ca * dm + r * (cp * x + cm * y)


def unsigned(parts, coef):
    dm, r, x, y = parts
    hr = 0.5 * r
    return coef * (jnp.abs(dm + hr * (x - y)) + hr * (x + y))


def kernel(
    dims, val_h, obst_h, slots_h, hor_h, off_h, tab_h, out,
    F, G, EX, Q, F1, G1, Q1, fail, obst, slots, hor, off, tab,
    lsem, ha_s, ha_r, y_s, y_r, x_s, x_r, dy_s, dy_r, dx_s, dx_r,
):
    nx, ny, nh, heads, sx, sy, sh, amax_x, amax_y, amax = dims
    gx, gy, ha = lax.axis_index("gx"), lax.axis_index("gy"), lax.axis_index("ha")
    ha_up = (gx, gy, lax.rem(ha + 1, nh))
    ha_dn = (gx, gy, lax.rem(ha + nh - 1, nh))
    y_up, y_dn = (gx, gy + 1, ha), (gx, gy - 1, ha)
    x_up, x_dn = (gx + 1, gy, ha), (gx - 1, gy, ha)
    has_yd, has_yu = gy > 0, gy < ny - 1
    has_xd, has_xu = gx > 0, gx < nx - 1

    bar = pltpu.get_barrier_semaphore()

    def signal(dev):
        pl.semaphore_signal(bar, inc=1, device_id=dev, device_id_type=MESH)

    signal(ha_up)
    signal(ha_dn)
    for cond, dev in ((has_yd, y_dn), (has_yu, y_up), (has_xd, x_dn), (has_xu, x_up)):
        pl.when(cond)(functools.partial(signal, dev))

    loads = [
        pltpu.make_async_copy(src, dst, lsem.at[i])
        for i, (src, dst) in enumerate(
            (
                (off_h, off), (hor_h, hor), (tab_h, tab), (slots_h, slots), (obst_h, obst),
                (val_h, F.at[:, pl.ds(4, 8)]),
            )
        )
    ]
    for load in loads:
        load.start()

    lane = lax.broadcasted_iota(jnp.int32, (8, 128), 1)
    sub = lax.broadcasted_iota(jnp.int32, (8, 128), 0)
    l8 = lane % 8
    low4 = l8 < 4
    grp = lane // 8

    def lroll(x, n):
        return pltpu.roll(x, n % 128, 1)

    def sroll(x, n):
        return pltpu.roll(x, n % 8, 0)

    for load in loads:
        load.wait()

    off0 = off[0]
    offf = off0.astype(f32)
    speeds = [speed_step * (offf + float(k)) for k in range(4)]
    smax = speed_step * jnp.maximum(jnp.abs(offf), jnp.abs(offf + 3.0))
    total = smax * amax + (turn_limit / sh + accel_limit / speed_step)
    dt = cfl_number / total
    spread_x, spread_y = smax * amax_x, smax * amax_y
    moment = hor[0] + dt

    def pack(base, tile_of, idx):
        e = EX[1, idx]
        for s in range(4):
            e = jnp.where(grp == base + s, lroll(tile_of(s), (base + s) * 8 + 4), e)
        EX[1, idx] = e

    def pack_main(h, _):
        pack(0, lambda s: F[s, h + 4], h + 2)
        return 0

    def pack_halo(h, _):
        pack(4, lambda s: G[s, h + 2], h + 2)
        return 0

    lax.fori_loop(0, 8, pack_main, 0)

    xv = ((gx * 128 + lane).astype(f32) + 0.5) * sx - half_width
    yv = ((gy * 8 + sub).astype(f32) + 0.5) * sy - half_width
    for g in range(2):
        cs = [tab[0, ha * 8 + g * 4 + j] for j in range(4)]
        sn = [tab[1, ha * 8 + g * 4 + j] for j in range(4)]

        def one(o, near, g=g, cs=cs, sn=sn):
            k = slots[g, o]
            cx = half_width * obst[0, k] + moment * (obstacle_speed * obst[2, k])
            cy = half_width * obst[1, k] + moment * (obstacle_speed * obst[3, k])
            reach = 1.25 + 0.75 * obst[4, k] + car_radius
            bx, by = xv - cx, yv - cy
            mid = bx * bx + by * by
            new = []
            for j in range(4):
                px, py = bx + cs[j], by + sn[j]
                qx, qy = bx - cs[j], by - sn[j]
                sq = jnp.minimum(mid, jnp.minimum(px * px + py * py, qx * qx + qy * qy))
                new.append(jnp.minimum(near[j], jnp.sqrt(sq) - reach))
            return tuple(new)

        far = jnp.full((8, 128), 3.0e38, f32)
        near = lax.fori_loop(0, SLOTS, one, (far,) * 4)
        for j in range(4):
            fail[g * 4 + j] = near[j]

    count = (
        2
        + jnp.where(has_yd, 1, 0) + jnp.where(has_yu, 1, 0)
        + jnp.where(has_xd, 1, 0) + jnp.where(has_xu, 1, 0)
    )
    pl.semaphore_wait(bar, count)

    def remote(src, dst, s, r, dev):
        return pltpu.make_async_remote_copy(
            src_ref=src, dst_ref=dst, send_sem=s, recv_sem=r, device_id=dev, device_id_type=MESH
        )

    ha_c = []
    for k in range(4):
        up = remote(F.at[:, 11 - k], F.at[:, 3 - k], ha_s.at[0, k], ha_r.at[0, k], ha_up)
        dn = remote(F.at[:, 4 + k], F.at[:, 12 + k], ha_s.at[1, k], ha_r.at[1, k], ha_dn)
        ha_c.append((up, dn))
    for up, dn in ha_c:
        up.start()
        dn.start()

    top, low = pl.ds(4, 4), pl.ds(0, 4)
    mine, near8 = pl.ds(4, 8), pl.ds(2, 8)
    yc_up = remote(F.at[:, mine, top], G.at[:, near8, top], y_s.at[0], y_r.at[0], y_up)
    yc_dn = remote(F.at[:, mine, low], G.at[:, near8, low], y_s.at[1], y_r.at[1], y_dn)
    pl.when(has_yu)(lambda: yc_up.start())
    pl.when(has_yd)(lambda: yc_dn.start())

    def fill_y(h, _):
        @pl.when(jnp.logical_not(has_yd))
        def _():
            for s in range(4):
                row = jnp.broadcast_to(F[s, h + 4, 0:1], (8, 128))
                G[s, h + 2] = jnp.where(sub >= 4, row, G[s, h + 2])

        @pl.when(jnp.logical_not(has_yu))
        def _():
            for s in range(4):
                row = jnp.broadcast_to(F[s, h + 4, 7:8], (8, 128))
                G[s, h + 2] = jnp.where(sub < 4, row, G[s, h + 2])

        return 0

    def fill_x(idx):
        @pl.when(jnp.logical_not(has_xd))
        def _():
            e = EX[1, idx]
            r = lroll(e, -4)
            for j in (1, 2, 3):
                r = jnp.where(l8 == j, lroll(e, j - 4), r)
            EX[0, idx] = r

        @pl.when(jnp.logical_not(has_xu))
        def _():
            e = EX[1, idx]
            r = lroll(e, 1)
            for j in (5, 6, 7):
                r = jnp.where(l8 == j, lroll(e, j - 3), r)
            EX[2, idx] = r

    def make_q(idx):
        left, own, right = EX[0, idx], EX[1, idx], EX[2, idx]
        a = jnp.where(low4, left, own)
        b = jnp.where(low4, own, right)
        Q[idx] = jnp.where(lane < 64, a, lroll(b, 64))

    pl.when(has_yd)(lambda: yc_up.wait_recv())
    pl.when(has_yu)(lambda: yc_dn.wait_recv())
    lax.fori_loop(0, 8, fill_y, 0)
    lax.fori_loop(0, 8, pack_halo, 0)

    xc_up = remote(EX.at[1, near8], EX.at[0, near8], x_s.at[0], x_r.at[0], x_up)
    xc_dn = remote(EX.at[1, near8], EX.at[2, near8], x_s.at[1], x_r.at[1], x_dn)
    pl.when(has_xu)(lambda: xc_up.start())
    pl.when(has_xd)(lambda: xc_dn.start())
    pl.when(has_xd)(lambda: xc_up.wait_recv())
    pl.when(has_xu)(lambda: xc_dn.wait_recv())

    def finish_x(h, _):
        fill_x(h + 2)
        make_q(h + 2)
        return 0

    lax.fori_loop(0, 8, finish_x, 0)

    eps = [weno_eps * s * s for s in (speed_step, sh, sy, sx)]
    k_v, k_h = 0.5 * accel_limit / speed_step, 0.5 * turn_limit / sh

    def coefs(alpha, spread, s):
        return (
            alpha * (0.5 / s), (spread + alpha) * (0.25 / s), (spread - alpha) * (0.25 / s)
        )

    def rate(vs, hs, ys, xs, along_x, along_y):
        acc = unsigned(sides(*vs, eps[0]), k_v) + unsigned(sides(*hs, eps[1]), k_h)
        acc = acc + upwind(sides(*ys, eps[2]), *coefs(along_y, spread_y, sy))
        acc = acc + upwind(sides(*xs, eps[3]), *coefs(along_x, spread_x, sx))
        return dt * jnp.minimum(0.0, acc)

    def y_five(z, other):
        return (
            sroll(jnp.where(sub >= 6, other, z), 2), sroll(jnp.where(sub == 7, other, z), 1), z,
            sroll(jnp.where(sub == 0, other, z), -1), sroll(jnp.where(sub < 2, other, z), -2),
        )

    def x_five(z, other):
        return (
            lroll(jnp.where(lane >= 126, other, z), 2), lroll(jnp.where(lane == 127, other, z), 1), z,
            lroll(jnp.where(lane == 0, other, z), -1), lroll(jnp.where(lane < 2, other, z), -2),
        )

    def clampi(i):
        return min(max(i, 0), 3)

    def turn(h):
        k = lax.rem(ha * 8 + h + heads, heads)
        return tab[0, k], tab[1, k]

    def stage(h, zs, hfive, others, halo, base):
        c, s_ = turn(h)
        res = []
        for s in range(4):
            vs = [zs[clampi(s + j)] for j in (-2, -1, 0, 1, 2)]
            edge = lroll(halo, -((base + s) * 8 + 4))
            res.append(
                zs[s]
                + rate(
                    vs, hfive(s), y_five(zs[s], others[s]), x_five(zs[s], edge),
                    speeds[s] * c, speeds[s] * s_,
                )
            )
        return res

    def one_main(h):
        zs = [F[s, h + 4] for s in range(4)]
        halo = jnp.where(low4, EX[0, h + 2], EX[2, h + 2])
        res = stage(
            h, zs, lambda s: [F[s, h + 4 + j] for j in (-2, -1, 0, 1, 2)],
            [G[s, h + 2] for s in range(4)], halo, 0,
        )
        for s in range(4):
            F1[s, h + 2] = res[s]

    def one_side(h):
        zs = [G[s, h + 2] for s in range(4)]
        halo = jnp.where(low4, EX[0, h + 2], EX[2, h + 2])
        res = stage(
            h, zs, lambda s: [G[s, h + 2 + j] for j in (-2, -1, 0, 1, 2)],
            [F[s, h + 4] for s in range(4)], halo, 4,
        )
        for s in range(4):
            G1[s, h] = res[s]
        z = Q[h + 2]
        s4 = grp % 4
        r8, l8_ = lroll(z, 8), lroll(z, -8)
        vs = (
            jnp.where(s4 == 0, z, jnp.where(s4 == 1, r8, lroll(z, 16))),
            jnp.where(s4 == 0, z, r8),
            z,
            jnp.where(s4 == 3, z, l8_),
            jnp.where(s4 == 3, z, jnp.where(s4 == 2, l8_, lroll(z, -16))),
        )
        swap = jnp.where(grp % 8 < 4, lroll(z, -32), lroll(z, 32))
        xs = (lroll(z, 2), lroll(z, 1), z, lroll(z, -1), lroll(z, -2))
        c, s_ = turn(h)
        sp = speed_step * (offf + s4.astype(f32))
        Q1[h] = z + rate(
            vs, [Q[h + 2 + j] for j in (-2, -1, 0, 1, 2)], y_five(z, swap), xs, sp * c, sp * s_
        )

    def early(i, _):
        one_main(i + 2)
        one_side(i + 2)
        return 0

    lax.fori_loop(0, 4, early, 0)

    pending = []
    for k in range(2):
        for d in range(2):
            ha_c[k][d].wait_recv()
            h = 8 + k if d else -1 - k
            row_up = remote(
                F.at[:, h + 4, top], G.at[:, h + 2, top], dy_s.at[0, d, k], dy_r.at[0, d, k], y_up
            )
            row_dn = remote(
                F.at[:, h + 4, low], G.at[:, h + 2, low], dy_s.at[1, d, k], dy_r.at[1, d, k], y_dn
            )
            pl.when(has_yu)(lambda c=row_up: c.start())
            pl.when(has_yd)(lambda c=row_dn: c.start())
            pack_main(h, 0)
            col_up = remote(
                EX.at[1, h + 2], EX.at[0, h + 2], dx_s.at[0, d, k], dx_r.at[0, d, k], x_up
            )
            col_dn = remote(
                EX.at[1, h + 2], EX.at[2, h + 2], dx_s.at[1, d, k], dx_r.at[1, d, k], x_dn
            )
            pl.when(has_xu)(lambda c=col_up: c.start())
            pl.when(has_xd)(lambda c=col_dn: c.start())
            pending.append((h, row_up, row_dn, col_up, col_dn))

    for h, row_up, row_dn, col_up, col_dn in pending:
        pl.when(has_yd)(lambda c=row_up: c.wait_recv())
        pl.when(has_yu)(lambda c=row_dn: c.wait_recv())
        pl.when(has_xd)(lambda c=col_up: c.wait_recv())
        pl.when(has_xu)(lambda c=col_dn: c.wait_recv())
        fill_y(h, 0)
        fill_x(h + 2)
        make_q(h + 2)

    def late_side(i, _):
        one_side(i + (i // 2) * 4)
        return 0

    lax.fori_loop(0, 4, late_side, 0)

    for k in range(2, 4):
        for d in range(2):
            ha_c[k][d].wait_recv()

    def late_main(i, _):
        one_main(i - 2 + (i // 4) * 4)
        return 0

    lax.fori_loop(0, 8, late_main, 0)

    @pl.when(jnp.logical_not(has_yd))
    def _():
        for h in range(8):
            for s in range(4):
                row = jnp.broadcast_to(F1[s, h + 2, 0:1], (8, 128))
                G1[s, h] = jnp.where(sub >= 4, row, G1[s, h])

    @pl.when(jnp.logical_not(has_yu))
    def _():
        for h in range(8):
            for s in range(4):
                row = jnp.broadcast_to(F1[s, h + 2, 7:8], (8, 128))
                G1[s, h] = jnp.where(sub < 4, row, G1[s, h])

    @pl.when(jnp.logical_not(has_xd))
    def _():
        for h in range(8):
            q = Q1[h]
            r = jnp.where(l8 == 3, lroll(q, -1), jnp.where(l8 == 2, lroll(q, -2), q))
            Q1[h] = jnp.where(lane < 64, r, q)

    @pl.when(jnp.logical_not(has_xu))
    def _():
        for h in range(8):
            q = Q1[h]
            r = jnp.where(l8 == 4, lroll(q, 1), jnp.where(l8 == 5, lroll(q, 2), q))
            Q1[h] = jnp.where(lane < 64, q, r)

    def second(h, _):
        zs = [F1[s, h + 2] for s in range(4)]
        q = Q1[h]
        halo = jnp.where(low4, q, lroll(q, 64))
        res = stage(
            h, zs, lambda s: [F1[s, h + 2 + j] for j in (-2, -1, 0, 1, 2)],
            [G1[s, h] for s in range(4)], halo, 0,
        )
        bound = fail[h]
        for s in range(4):
            out[s, h] = jnp.minimum(0.5 * (F[s, h + 4] + res[s]), bound)
        return 0

    lax.fori_loop(0, 8, second, 0)

    for up, dn in ha_c:
        up.wait_send()
        dn.wait_send()
    pl.when(has_yu)(lambda: yc_up.wait_send())
    pl.when(has_yd)(lambda: yc_dn.wait_send())
    pl.when(has_xu)(lambda: xc_up.wait_send())
    pl.when(has_xd)(lambda: xc_dn.wait_send())
    for h, row_up, row_dn, col_up, col_dn in pending:
        pl.when(has_yu)(lambda c=row_up: c.wait_send())
        pl.when(has_yd)(lambda c=row_dn: c.wait_send())
        pl.when(has_xu)(lambda c=col_up: c.wait_send())
        pl.when(has_xd)(lambda c=col_dn: c.wait_send())


def solution(mesh):
    nx, ny, nh = mesh.shape["gx"], mesh.shape["gy"], mesh.shape["ha"]
    in_specs = (P(None, "ha", "gy", "gx"), P(), P("ha", None), P(), P())
    out_specs = P(None, "ha", "gy", "gx")

    def local(value, obstacles, obstacle_slots, horizon, speed_offset):
        heads = value.shape[1] * nh
        sx = 2.0 * half_width / (value.shape[3] * nx)
        sy = 2.0 * half_width / (value.shape[2] * ny)
        sh = 2.0 * math.pi / heads
        cos, sin = grid_tables(heads)
        c64, s64 = np.abs(cos.astype(np.float64)), np.abs(sin.astype(np.float64))
        dims = (
            nx, ny, nh, heads, sx, sy, sh,
            float(c64.max()), float(s64.max()), float((c64 / sx + s64 / sy).max()),
        )
        anyspec = pl.BlockSpec(memory_space=pl.ANY)
        vm, dma = pltpu.VMEM, pltpu.SemaphoreType.DMA
        return pl.pallas_call(
            functools.partial(kernel, dims),
            out_shape=jax.ShapeDtypeStruct(value.shape, f32),
            in_specs=[anyspec] * 6,
            out_specs=pl.BlockSpec(memory_space=pltpu.VMEM),
            scratch_shapes=[
                vm((4, 16, 8, 128), f32), vm((4, 12, 8, 128), f32), vm((3, 12, 8, 128), f32),
                vm((12, 8, 128), f32), vm((4, 12, 8, 128), f32), vm((4, 8, 8, 128), f32),
                vm((8, 8, 128), f32), vm((8, 8, 128), f32),
                pltpu.SMEM((5, 128), f32), pltpu.SMEM((2, 16), jnp.int32),
                pltpu.SMEM((1,), f32), pltpu.SMEM((1,), jnp.int32), pltpu.SMEM((2, 64), f32),
                dma((6,)), dma((2, 4)), dma((2, 4)), dma((2,)), dma((2,)), dma((2,)), dma((2,)),
                dma((2, 2, 2)), dma((2, 2, 2)), dma((2, 2, 2)), dma((2, 2, 2)),
            ],
            compiler_params=pltpu.CompilerParams(
                collective_id=0, has_side_effects=True, vmem_limit_bytes=16 * 2**20
            ),
            name="tube_step",
        )(value, obstacles, obstacle_slots, horizon, speed_offset, jnp.asarray(np.stack([cos, sin])))

    return jax.shard_map(
        local, mesh=mesh, in_specs=in_specs, out_specs=out_specs, check_vma=False
    )
```

time: 86.1 us -> 47.3 us (0.55)
  Pallas kernels: 0 us -> 43.5 us
  starting transfers between devices: 31.4 us -> 0 us
  other arithmetic: 25.6 us -> 0 us
  waiting for transfers between devices: 12.4 us -> 0 us
  local copies, waits for them, and re-layouts: 13.8 us -> 2.25 us
  between operations: 2.32 us -> 1.37 us
    pallas_call x0 -> x1, Pallas kernels: none -> 43.5 us  [local(): pl.pallas_call(functools.partial(kernel, dims), out_shape=jax.ShapeDtypeS...]
    ppermute x6 -> x0, starting transfers between devices: 31.4 us -> none  [the longest x3 24.1 us: extended_2(): before = lax.ppermute(last, axis, up)]
    add x7 -> x0, other arithmetic: 13.9 us -> none  [the longest x1 11.8 us: advance_box(): inner + time_step * hamiltonian_rate(pieces, speeds, angles, (spread_x, s...]
    ppermute x6 -> x0, waiting for transfers between devices: 12.4 us -> none  [the longest x3 7.77 us: extended_2(): after = lax.ppermute(initial, axis, down)]
    select_n x12 -> x0, other arithmetic: 5.5 us -> none  [the longest x2 1.5 us: group_field(): centre_x = jnp.take(centre_x, slot_row)[None, :, None, None]]
    slice x13 -> x0, local copies, waits for them, and re-layouts: 4.36 us -> none  [the longest x2 0.96 us: extended_2(): initial = lax.slice_in_dim(value, 0, width, axis=dim)]
    gather x6 -> x0, local copies, waits for them, and re-layouts: 3.98 us -> none  [the longest x2 1.33 us: group_field(): centre_x = jnp.take(centre_x, slot_row)[None, :, None, None]]
    min x1 -> x0, other arithmetic: 3.68 us -> none  [local(): return jnp.minimum(0.5 * (value + section_two), failure[None])]
  transfers between devices with their start and end apart: 6 -> 0, of which waited for: 4 -> 0; matrix products, arithmetic and copies ran while one was open for 12% -> 0% of each run, Pallas kernels for 0% -> 0%
where the time goes in v1:
time: 47.3 us; the launch traced here: 47.1 us
  Pallas kernels  43.5 us (92%)
  local copies, waits for them, and re-layouts  2.25 us (5%)
  between operations  1.37 us (3%)
    pallas_call x1, Pallas kernels, local(): pl.pallas_call(functools.partial(kernel, dims), out_shape=jax.ShapeDtypeS...  43.5 us
    unnamed x9, local copies, waits for them, and re-layouts  2.25 us

profile of v1, /device:TPU:1, one launch (start us, length us, event | category | flops | bytes accessed | tf_op | source)
XLA Modules:
  0.0 47.1 jit_solution(4333714752620682482)
XLA Ops:
  0.0 0.0 copy-start.3
  0.7 0.0 copy-start.2
  1.3 0.0 copy-done.3
  1.3 0.0 copy-done.2
  1.4 0.0 copy-start
  1.4 0.9 %copy-done = f32[4,8,8,128]{3,2,1,0:T(8,128)S(1)} copy-done((f32[4,8,8,128]{3,2,1,0:T(8,128)S(1)}, f32[4,8,8,128]{3,2,1,0:T(8,128)}, u32[]{:S(2)}) %copy-start) | copy-done | bytes 131096
  2.3 0.0 copy-start.1
  2.3 0.7 %copy-done.1 = f32[5,128]{1,0:T(8,128)S(1)} copy-done((f32[5,128]{1,0:T(8,128)S(1)}, f32[5,128]{1,0:T(8,128)}, u32[]{:S(2)}) %copy-start.1) | copy-done | bytes 2584
  2.9 43.5 %tube_step.1 = f32[4,8,8,128]{3,2,1,0:T(8,128)S(1)} custom-call(f32[4,8,8,128]{3,2,1,0:T(8,128)S(1)} %copy-done, f32[5,128]{1,0:T(8,128)S(1)} %copy-done.1, s32[2,16]{1,0:T(2,128)S(1)} %copy-done.2, f32[1]{0:T(128)S(6)} %copy.8.hor_h, s32[1]{0:T(128)S(6)} %copy.9.off_h, f32[2,64]{1,0:T(2,128)S(1)} %copy-done.3), custom_call_target="tpu_custom_call" | custom-call | tf_op jit(solution)/shard_map/tube_step/pallas_call | solution.py:457
  46.5 0.7 %copy.10 = f32[4,8,8,128]{3,2,1,0:T(8,128)} copy(f32[4,8,8,128]{3,2,1,0:T(8,128)S(1)} %tube_step.1) | data formatting | bytes 262144
Async XLA Ops:
  0.0 1.3 %copy-start.3 = (f32[2,64]{1,0:T(2,128)S(1)}, f32[2,64]{1,0:T(2,128)}, u32[]{:S(2)}) copy-start(f32[2,64]{1,0:T(2,128)} %constant.2.clone.tab_h) | copy-start | bytes 1540
  0.7 0.7 %copy-start.2 = (s32[2,16]{1,0:T(2,128)S(1)}, s32[2,16]{1,0:T(2,128)}, u32[]{:S(2)}) copy-start(s32[2,16]{1,0:T(2,128)} %slots_h.1) | copy-start | bytes 388
  1.4 0.9 %copy-start = (f32[4,8,8,128]{3,2,1,0:T(8,128)S(1)}, f32[4,8,8,128]{3,2,1,0:T(8,128)}, u32[]{:S(2)}) copy-start(f32[4,8,8,128]{3,2,1,0:T(8,128)} %val_h.1) | copy-start | bytes 393220
  2.3 0.7 %copy-start.1 = (f32[5,128]{1,0:T(8,128)S(1)}, f32[5,128]{1,0:T(8,128)}, u32[]{:S(2)}) copy-start(f32[5,128]{1,0:T(8,128)} %obst_h.1) | copy-start | bytes 7684

commit v2 on v1

--- a/solution.py
+++ b/solution.py
@@ -99,6 +99,34 @@
     def sroll(x, n):
         return pltpu.roll(x, n % 8, 0)
 
+    count = (
+        2
+        + jnp.where(has_yd, 1, 0) + jnp.where(has_yu, 1, 0)
+        + jnp.where(has_xd, 1, 0) + jnp.where(has_xu, 1, 0)
+    )
+    pl.semaphore_wait(bar, count)
+
+    def remote(src, dst, s, r, dev):
+        return pltpu.make_async_remote_copy(
+            src_ref=src, dst_ref=dst, send_sem=s, recv_sem=r, device_id=dev, device_id_type=MESH
+        )
+
+    top, low = pl.ds(4, 4), pl.ds(0, 4)
+    near8 = pl.ds(2, 8)
+    yc_up = remote(val_h.at[:, :, top], G.at[:, near8, top], y_s.at[0], y_r.at[0], y_up)
+    yc_dn = remote(val_h.at[:, :, low], G.at[:, near8, low], y_s.at[1], y_r.at[1], y_dn)
+    pl.when(has_yu)(lambda: yc_up.start())
+    pl.when(has_yd)(lambda: yc_dn.start())
+
+    ha_c = []
+    for k in range(4):
+        up = remote(val_h.at[:, 7 - k], F.at[:, 3 - k], ha_s.at[0, k], ha_r.at[0, k], ha_up)
+        dn = remote(val_h.at[:, k], F.at[:, 12 + k], ha_s.at[1, k], ha_r.at[1, k], ha_dn)
+        ha_c.append((up, dn))
+    for up, dn in ha_c[:2]:
+        up.start()
+        dn.start()
+
     for load in loads:
         load.wait()
 
@@ -125,61 +153,32 @@
         pack(4, lambda s: G[s, h + 2], h + 2)
         return 0
 
-    lax.fori_loop(0, 8, pack_main, 0)
-
-    xv = ((gx * 128 + lane).astype(f32) + 0.5) * sx - half_width
-    yv = ((gy * 8 + sub).astype(f32) + 0.5) * sy - half_width
-    for g in range(2):
-        cs = [tab[0, ha * 8 + g * 4 + j] for j in range(4)]
-        sn = [tab[1, ha * 8 + g * 4 + j] for j in range(4)]
-
-        def one(o, near, g=g, cs=cs, sn=sn):
-            k = slots[g, o]
-            cx = half_width * obst[0, k] + moment * (obstacle_speed * obst[2, k])
-            cy = half_width * obst[1, k] + moment * (obstacle_speed * obst[3, k])
-            reach = 1.25 + 0.75 * obst[4, k] + car_radius
-            bx, by = xv - cx, yv - cy
-            mid = bx * bx + by * by
-            new = []
+    def failure_field():
+        xv = ((gx * 128 + lane).astype(f32) + 0.5) * sx - half_width
+        yv = ((gy * 8 + sub).astype(f32) + 0.5) * sy - half_width
+        for g in range(2):
+            cs = [tab[0, ha * 8 + g * 4 + j] for j in range(4)]
+            sn = [tab[1, ha * 8 + g * 4 + j] for j in range(4)]
+
+            def one(o, near, g=g, cs=cs, sn=sn):
+                k = slots[g, o]
+                cx = half_width * obst[0, k] + moment * (obstacle_speed * obst[2, k])
+                cy = half_width * obst[1, k] + moment * (obstacle_speed * obst[3, k])
+                reach = 1.25 + 0.75 * obst[4, k] + car_radius
+                bx, by = xv - cx, yv - cy
+                mid = bx * bx + by * by
+                new = []
+                for j in range(4):
+                    px, py = bx + cs[j], by + sn[j]
+                    qx, qy = bx - cs[j], by - sn[j]
+                    sq = jnp.minimum(mid, jnp.minimum(px * px + py * py, qx * qx + qy * qy))
+                    new.append(jnp.minimum(near[j], jnp.sqrt(sq) - reach))
+                return tuple(new)
+
+            far = jnp.full((8, 128), 3.0e38, f32)
+            near = lax.fori_loop(0, SLOTS, one, (far,) * 4)
             for j in range(4):
-                px, py = bx + cs[j], by + sn[j]
-                qx, qy = bx - cs[j], by - sn[j]
-                sq = jnp.minimum(mid, jnp.minimum(px * px + py * py, qx * qx + qy * qy))
-                new.append(jnp.minimum(near[j], jnp.sqrt(sq) - reach))
-            return tuple(new)
-
-        far = jnp.full((8, 128), 3.0e38, f32)
-        near = lax.fori_loop(0, SLOTS, one, (far,) * 4)
-        for j in range(4):
-            fail[g * 4 + j] = near[j]
-
-    count = (
-        2
-        + jnp.where(has_yd, 1, 0) + jnp.where(has_yu, 1, 0)
-        + jnp.where(has_xd, 1, 0) + jnp.where(has_xu, 1, 0)
-    )
-    pl.semaphore_wait(bar, count)
-
-    def remote(src, dst, s, r, dev):
-        return pltpu.make_async_remote_copy(
-            src_ref=src, dst_ref=dst, send_sem=s, recv_sem=r, device_id=dev, device_id_type=MESH
-        )
-
-    ha_c = []
-    for k in range(4):
-        up = remote(F.at[:, 11 - k], F.at[:, 3 - k], ha_s.at[0, k], ha_r.at[0, k], ha_up)
-        dn = remote(F.at[:, 4 + k], F.at[:, 12 + k], ha_s.at[1, k], ha_r.at[1, k], ha_dn)
-        ha_c.append((up, dn))
-    for up, dn in ha_c:
-        up.start()
-        dn.start()
-
-    top, low = pl.ds(4, 4), pl.ds(0, 4)
-    mine, near8 = pl.ds(4, 8), pl.ds(2, 8)
-    yc_up = remote(F.at[:, mine, top], G.at[:, near8, top], y_s.at[0], y_r.at[0], y_up)
-    yc_dn = remote(F.at[:, mine, low], G.at[:, near8, low], y_s.at[1], y_r.at[1], y_dn)
-    pl.when(has_yu)(lambda: yc_up.start())
-    pl.when(has_yd)(lambda: yc_dn.start())
+                fail[g * 4 + j] = near[j]
 
     def fill_y(h, _):
         @pl.when(jnp.logical_not(has_yd))
@@ -219,8 +218,12 @@
         b = jnp.where(low4, own, right)
         Q[idx] = jnp.where(lane < 64, a, lroll(b, 64))
 
+    lax.fori_loop(0, 8, pack_main, 0)
     pl.when(has_yd)(lambda: yc_up.wait_recv())
     pl.when(has_yu)(lambda: yc_dn.wait_recv())
+    for up, dn in ha_c[2:]:
+        up.start()
+        dn.start()
     lax.fori_loop(0, 8, fill_y, 0)
     lax.fori_loop(0, 8, pack_halo, 0)
 
@@ -228,6 +231,7 @@
     xc_dn = remote(EX.at[1, near8], EX.at[2, near8], x_s.at[1], x_r.at[1], x_dn)
     pl.when(has_xu)(lambda: xc_up.start())
     pl.when(has_xd)(lambda: xc_dn.start())
+    failure_field()
     pl.when(has_xd)(lambda: xc_up.wait_recv())
     pl.when(has_xu)(lambda: xc_dn.wait_recv())
 
@@ -323,6 +327,44 @@
             vs, [Q[h + 2 + j] for j in (-2, -1, 0, 1, 2)], y_five(z, swap), xs, sp * c, sp * s_
         )
 
+    def fix_edges(h):
+        @pl.when(jnp.logical_not(has_yd))
+        def _():
+            for s in range(4):
+                row = jnp.broadcast_to(F1[s, h + 2, 0:1], (8, 128))
+                G1[s, h] = jnp.where(sub >= 4, row, G1[s, h])
+
+        @pl.when(jnp.logical_not(has_yu))
+        def _():
+            for s in range(4):
+                row = jnp.broadcast_to(F1[s, h + 2, 7:8], (8, 128))
+                G1[s, h] = jnp.where(sub < 4, row, G1[s, h])
+
+        @pl.when(jnp.logical_not(has_xd))
+        def _():
+            q = Q1[h]
+            r = jnp.where(l8 == 3, lroll(q, -1), jnp.where(l8 == 2, lroll(q, -2), q))
+            Q1[h] = jnp.where(lane < 64, r, q)
+
+        @pl.when(jnp.logical_not(has_xu))
+        def _():
+            q = Q1[h]
+            r = jnp.where(l8 == 4, lroll(q, 1), jnp.where(l8 == 5, lroll(q, 2), q))
+            Q1[h] = jnp.where(lane < 64, q, r)
+
+    def second(h):
+        fix_edges(h)
+        zs = [F1[s, h + 2] for s in range(4)]
+        q = Q1[h]
+        halo = jnp.where(low4, q, lroll(q, 64))
+        res = stage(
+            h, zs, lambda s: [F1[s, h + 2 + j] for j in (-2, -1, 0, 1, 2)],
+            [G1[s, h] for s in range(4)], halo, 0,
+        )
+        bound = fail[h]
+        for s in range(4):
+            out[s, h] = jnp.minimum(0.5 * (F[s, h + 4] + res[s]), bound)
+
     def early(i, _):
         one_main(i + 2)
         one_side(i + 2)
@@ -353,6 +395,17 @@
             pl.when(has_xu)(lambda c=col_up: c.start())
             pl.when(has_xd)(lambda c=col_dn: c.start())
             pending.append((h, row_up, row_dn, col_up, col_dn))
+
+    def inner_main(i, _):
+        one_main(i + (i // 2) * 4)
+        return 0
+
+    def inner_second(i, _):
+        second(i + 2)
+        return 0
+
+    lax.fori_loop(0, 4, inner_main, 0)
+    lax.fori_loop(0, 4, inner_second, 0)
 
     for h, row_up, row_dn, col_up, col_dn in pending:
         pl.when(has_yd)(lambda c=row_up: c.wait_recv())
@@ -374,53 +427,15 @@
             ha_c[k][d].wait_recv()
 
     def late_main(i, _):
-        one_main(i - 2 + (i // 4) * 4)
-        return 0
-
-    lax.fori_loop(0, 8, late_main, 0)
-
-    @pl.when(jnp.logical_not(has_yd))
-    def _():
-        for h in range(8):
-            for s in range(4):
-                row = jnp.broadcast_to(F1[s, h + 2, 0:1], (8, 128))
-                G1[s, h] = jnp.where(sub >= 4, row, G1[s, h])
-
-    @pl.when(jnp.logical_not(has_yu))
-    def _():
-        for h in range(8):
-            for s in range(4):
-                row = jnp.broadcast_to(F1[s, h + 2, 7:8], (8, 128))
-                G1[s, h] = jnp.where(sub < 4, row, G1[s, h])
-
-    @pl.when(jnp.logical_not(has_xd))
-    def _():
-        for h in range(8):
-            q = Q1[h]
-            r = jnp.where(l8 == 3, lroll(q, -1), jnp.where(l8 == 2, lroll(q, -2), q))
-            Q1[h] = jnp.where(lane < 64, r, q)
-
-    @pl.when(jnp.logical_not(has_xu))
-    def _():
-        for h in range(8):
-            q = Q1[h]
-            r = jnp.where(l8 == 4, lroll(q, 1), jnp.where(l8 == 5, lroll(q, 2), q))
-            Q1[h] = jnp.where(lane < 64, q, r)
-
-    def second(h, _):
-        zs = [F1[s, h + 2] for s in range(4)]
-        q = Q1[h]
-        halo = jnp.where(low4, q, lroll(q, 64))
-        res = stage(
-            h, zs, lambda s: [F1[s, h + 2 + j] for j in (-2, -1, 0, 1, 2)],
-            [G1[s, h] for s in range(4)], halo, 0,
-        )
-        bound = fail[h]
-        for s in range(4):
-            out[s, h] = jnp.minimum(0.5 * (F[s, h + 4] + res[s]), bound)
-        return 0
-
-    lax.fori_loop(0, 8, second, 0)
+        one_main(i - 2 + (i // 2) * 8)
+        return 0
+
+    def late_second(i, _):
+        second(i + (i // 2) * 4)
+        return 0
+
+    lax.fori_loop(0, 4, late_main, 0)
+    lax.fori_loop(0, 4, late_second, 0)
 
     for up, dn in ha_c:
         up.wait_send()
@@ -452,12 +467,12 @@
             nx, ny, nh, heads, sx, sy, sh,
             float(c64.max()), float(s64.max()), float((c64 / sx + s64 / sy).max()),
         )
-        anyspec = pl.BlockSpec(memory_space=pl.ANY)
+        anyspec = pl.BlockSpec(memory_space=pltpu.HBM)
         vm, dma = pltpu.VMEM, pltpu.SemaphoreType.DMA
         return pl.pallas_call(
             functools.partial(kernel, dims),
             out_shape=jax.ShapeDtypeStruct(value.shape, f32),
-            in_specs=[anyspec] * 6,
+            in_specs=[anyspec] * 3 + [pl.BlockSpec(memory_space=pl.ANY)] * 2 + [anyspec],
             out_specs=pl.BlockSpec(memory_space=pltpu.VMEM),
             scratch_shapes=[
                 vm((4, 16, 8, 128), f32), vm((4, 12, 8, 128), f32), vm((3, 12, 8, 128), f32),
@@ -472,7 +487,13 @@
                 collective_id=0, has_side_effects=True, vmem_limit_bytes=16 * 2**20
             ),
             name="tube_step",
-        )(value, obstacles, obstacle_slots, horizon, speed_offset, jnp.asarray(np.stack([cos, sin])))
+        )(*(
+            x if x.size == 1 else pltpu.with_memory_space_constraint(x, pltpu.HBM)
+            for x in (
+                value, obstacles, obstacle_slots, horizon, speed_offset,
+                jnp.asarray(np.stack([cos, sin])),
+            )
+        ))
 
     return jax.shard_map(
         local, mesh=mesh, in_specs=in_specs, out_specs=out_specs, check_vma=False

time: 47.3 us -> 36.4 us (0.77)
  the two profiles are of different devices: /device:TPU:1 before, /device:TPU:17 now
where the time goes in v2:
time: 36.4 us; the launch traced here: 36.3 us
  Pallas kernels  34.3 us (94%)
  between operations  1.3 us (4%)
  local copies, waits for them, and re-layouts  0.66 us (2%)
    pallas_call x1, Pallas kernels, local(): pl.pallas_call(functools.partial(kernel, dims), out_shape=jax.ShapeDtypeS...  34.3 us

profile of v2, /device:TPU:17, one launch (start us, length us, event | category | flops | bytes accessed | tf_op | source)
XLA Modules:
  0.0 36.3 jit_solution(12551862449278960454)
XLA Ops:
  1.3 34.3 %tube_step.1 = f32[4,8,8,128]{3,2,1,0:T(8,128)S(1)} custom-call(f32[4,8,8,128]{3,2,1,0:T(8,128)} %val_h.1, f32[5,128]{1,0:T(8,128)} %obst_h.1, s32[2,16]{1,0:T(2,128)} %slots_h.1, f32[1]{0:T(128)S(6)} %copy.8.hor_h, s32[1]{0:T(128)S(6)} %copy.9.off_h, f32[2,64]{1,0:T(2,128)} %constant.2.clone.tab_h), custom_call_target="tpu_custom_call" | custom-call | tf_op jit(solution)/shard_map/tube_step/pallas_call | solution.py:472
  35.6 0.7 %copy.10 = f32[4,8,8,128]{3,2,1,0:T(8,128)} copy(f32[4,8,8,128]{3,2,1,0:T(8,128)S(1)} %tube_step.1) | data formatting | bytes 262144

commit v3 on v2

--- a/solution.py
+++ b/solution.py
@@ -35,7 +35,8 @@
     u, v, w = d2 - d1, d3 - d2, d4 - d3
     a, b, c = eps + u * u, eps + v * v, eps + w * w
     a, b, c = a * a, b * b, c * c
-    p, q = b + (a + a), b + (c + c)
+    b = 0.5 * b
+    p, q = b + a, b + c
     r = b / (p * q)
     return p1 - m1, r, (u - v) * q, (w - v) * p
 
@@ -79,8 +80,8 @@
         pltpu.make_async_copy(src, dst, lsem.at[i])
         for i, (src, dst) in enumerate(
             (
-                (off_h, off), (hor_h, hor), (tab_h, tab), (slots_h, slots), (obst_h, obst),
-                (val_h, F.at[:, pl.ds(4, 8)]),
+                (val_h, F.at[:, pl.ds(4, 8)]), (off_h, off), (hor_h, hor), (tab_h, tab),
+                (slots_h, slots), (obst_h, obst),
             )
         )
     ]
@@ -104,6 +105,7 @@
         + jnp.where(has_yd, 1, 0) + jnp.where(has_yu, 1, 0)
         + jnp.where(has_xd, 1, 0) + jnp.where(has_xu, 1, 0)
     )
+    loads[0].wait()
     pl.semaphore_wait(bar, count)
 
     def remote(src, dst, s, r, dev):
@@ -112,22 +114,22 @@
         )
 
     top, low = pl.ds(4, 4), pl.ds(0, 4)
-    near8 = pl.ds(2, 8)
-    yc_up = remote(val_h.at[:, :, top], G.at[:, near8, top], y_s.at[0], y_r.at[0], y_up)
-    yc_dn = remote(val_h.at[:, :, low], G.at[:, near8, low], y_s.at[1], y_r.at[1], y_dn)
+    mine, near8 = pl.ds(4, 8), pl.ds(2, 8)
+    yc_up = remote(F.at[:, mine, top], G.at[:, near8, top], y_s.at[0], y_r.at[0], y_up)
+    yc_dn = remote(F.at[:, mine, low], G.at[:, near8, low], y_s.at[1], y_r.at[1], y_dn)
     pl.when(has_yu)(lambda: yc_up.start())
     pl.when(has_yd)(lambda: yc_dn.start())
 
     ha_c = []
     for k in range(4):
-        up = remote(val_h.at[:, 7 - k], F.at[:, 3 - k], ha_s.at[0, k], ha_r.at[0, k], ha_up)
-        dn = remote(val_h.at[:, k], F.at[:, 12 + k], ha_s.at[1, k], ha_r.at[1, k], ha_dn)
+        up = remote(F.at[:, 11 - k], F.at[:, 3 - k], ha_s.at[0, k], ha_r.at[0, k], ha_up)
+        dn = remote(F.at[:, 4 + k], F.at[:, 12 + k], ha_s.at[1, k], ha_r.at[1, k], ha_dn)
         ha_c.append((up, dn))
     for up, dn in ha_c[:2]:
         up.start()
         dn.start()
 
-    for load in loads:
+    for load in loads[1:]:
         load.wait()
 
     off0 = off[0]
@@ -378,10 +380,10 @@
             ha_c[k][d].wait_recv()
             h = 8 + k if d else -1 - k
             row_up = remote(
-                F.at[:, h + 4, top], G.at[:, h + 2, top], dy_s.at[0, d, k], dy_r.at[0, d, k], y_up
+                F.at[:, h + 4, pl.ds(6, 2)], G.at[:, h + 2, pl.ds(6, 2)], dy_s.at[0, d, k], dy_r.at[0, d, k], y_up
             )
             row_dn = remote(
-                F.at[:, h + 4, low], G.at[:, h + 2, low], dy_s.at[1, d, k], dy_r.at[1, d, k], y_dn
+                F.at[:, h + 4, pl.ds(0, 2)], G.at[:, h + 2, pl.ds(0, 2)], dy_s.at[1, d, k], dy_r.at[1, d, k], y_dn
             )
             pl.when(has_yu)(lambda c=row_up: c.start())
             pl.when(has_yd)(lambda c=row_dn: c.start())
@@ -420,7 +422,7 @@
         one_side(i + (i // 2) * 4)
         return 0
 
-    lax.fori_loop(0, 4, late_side, 0)
+    lax.fori_loop(0, 4, late_side, 0, unroll=4)
 
     for k in range(2, 4):
         for d in range(2):
@@ -434,8 +436,8 @@
         second(i + (i // 2) * 4)
         return 0
 
-    lax.fori_loop(0, 4, late_main, 0)
-    lax.fori_loop(0, 4, late_second, 0)
+    lax.fori_loop(0, 4, late_main, 0, unroll=4)
+    lax.fori_loop(0, 4, late_second, 0, unroll=4)
 
     for up, dn in ha_c:
         up.wait_send()

time: 36.4 us -> 35.3 us (0.970)
  Pallas kernels: 34.3 us -> 33.2 us
    pallas_call x1, Pallas kernels: 34.3 us -> 33.2 us  [local(): pl.pallas_call(functools.partial(kernel, dims), out_shape=jax.ShapeDtypeS...]
where the time goes in v3:
time: 35.3 us; the launch traced here: 35.2 us
  Pallas kernels  33.2 us (94%)
  between operations  1.3 us (4%)
  local copies, waits for them, and re-layouts  0.66 us (2%)
    pallas_call x1, Pallas kernels, local(): pl.pallas_call(functools.partial(kernel, dims), out_shape=jax.ShapeDtypeS...  33.2 us

profile of v3, /device:TPU:17, one launch (start us, length us, event | category | flops | bytes accessed | tf_op | source)
XLA Modules:
  0.0 35.2 jit_solution(280027754054008965)
XLA Ops:
  1.3 33.2 %tube_step.1 = f32[4,8,8,128]{3,2,1,0:T(8,128)S(1)} custom-call(f32[4,8,8,128]{3,2,1,0:T(8,128)} %val_h.1, f32[5,128]{1,0:T(8,128)} %obst_h.1, s32[2,16]{1,0:T(2,128)} %slots_h.1, f32[1]{0:T(128)S(6)} %copy.8.hor_h, s32[1]{0:T(128)S(6)} %copy.9.off_h, f32[2,64]{1,0:T(2,128)} %constant.2.clone.tab_h), custom_call_target="tpu_custom_call" | custom-call | tf_op jit(solution)/shard_map/tube_step/pallas_call | solution.py:474
  34.5 0.7 %copy.10 = f32[4,8,8,128]{3,2,1,0:T(8,128)} copy(f32[4,8,8,128]{3,2,1,0:T(8,128)S(1)} %tube_step.1) | data formatting | bytes 262144

commit v4 on v3

--- a/solution.py
+++ b/solution.py
@@ -121,10 +121,13 @@
     pl.when(has_yd)(lambda: yc_dn.start())
 
     ha_c = []
-    for k in range(4):
+    for k in range(2):
         up = remote(F.at[:, 11 - k], F.at[:, 3 - k], ha_s.at[0, k], ha_r.at[0, k], ha_up)
         dn = remote(F.at[:, 4 + k], F.at[:, 12 + k], ha_s.at[1, k], ha_r.at[1, k], ha_dn)
         ha_c.append((up, dn))
+    up = remote(F.at[:, pl.ds(8, 2)], F.at[:, pl.ds(0, 2)], ha_s.at[0, 2], ha_r.at[0, 2], ha_up)
+    dn = remote(F.at[:, pl.ds(6, 2)], F.at[:, pl.ds(14, 2)], ha_s.at[1, 2], ha_r.at[1, 2], ha_dn)
+    ha_c.append((up, dn))
     for up, dn in ha_c[:2]:
         up.start()
         dn.start()
@@ -372,7 +375,7 @@
         one_side(i + 2)
         return 0
 
-    lax.fori_loop(0, 4, early, 0)
+    lax.fori_loop(0, 4, early, 0, unroll=4)
 
     pending = []
     for k in range(2):
@@ -406,8 +409,8 @@
         second(i + 2)
         return 0
 
-    lax.fori_loop(0, 4, inner_main, 0)
-    lax.fori_loop(0, 4, inner_second, 0)
+    lax.fori_loop(0, 4, inner_main, 0, unroll=4)
+    lax.fori_loop(0, 4, inner_second, 0, unroll=4)
 
     for h, row_up, row_dn, col_up, col_dn in pending:
         pl.when(has_yd)(lambda c=row_up: c.wait_recv())
@@ -424,9 +427,8 @@
 
     lax.fori_loop(0, 4, late_side, 0, unroll=4)
 
-    for k in range(2, 4):
-        for d in range(2):
-            ha_c[k][d].wait_recv()
+    for d in range(2):
+        ha_c[2][d].wait_recv()
 
     def late_main(i, _):
         one_main(i - 2 + (i // 2) * 8)

time: 35.3 us -> 35.3 us (level)
  no operation moved by 1% of the time
where the time goes in v4:
time: 35.3 us; the launch traced here: 35.2 us
  Pallas kernels  33.2 us (94%)
  between operations  1.3 us (4%)
  local copies, waits for them, and re-layouts  0.66 us (2%)
    pallas_call x1, Pallas kernels, local(): pl.pallas_call(functools.partial(kernel, dims), out_shape=jax.ShapeDtypeS...  33.2 us

profile of v4, /device:TPU:17, one launch (start us, length us, event | category | flops | bytes accessed | tf_op | source)
XLA Modules:
  0.0 35.2 jit_solution(12528605299667458759)
XLA Ops:
  1.3 33.2 %tube_step.1 = f32[4,8,8,128]{3,2,1,0:T(8,128)S(1)} custom-call(f32[4,8,8,128]{3,2,1,0:T(8,128)} %val_h.1, f32[5,128]{1,0:T(8,128)} %obst_h.1, s32[2,16]{1,0:T(2,128)} %slots_h.1, f32[1]{0:T(128)S(6)} %copy.8.hor_h, s32[1]{0:T(128)S(6)} %copy.9.off_h, f32[2,64]{1,0:T(2,128)} %constant.2.clone.tab_h), custom_call_target="tpu_custom_call" | custom-call | tf_op jit(solution)/shard_map/tube_step/pallas_call | solution.py:476
  34.5 0.7 %copy.10 = f32[4,8,8,128]{3,2,1,0:T(8,128)} copy(f32[4,8,8,128]{3,2,1,0:T(8,128)S(1)} %tube_step.1) | data formatting | bytes 262144
